TPU v7x, 32 devices: a whole 2x2x4 slice. The times are simulated.
32 devices in a mesh: dp: 8 (over y, x, core), mp: 4 (over z).
Axes of the slice: x: 2, y: 2, z: 4, core: 2. Of those that a mesh axis runs over, the one named last changes fastest.
Arguments:
- tokens: bfloat16 [64, 256, 1024], P(('dp', 'mp')), may hold values from -6 to 6
- cotangent: bfloat16 [64, 256, 1024], P(('dp', 'mp')), may hold values from -6 to 6
- w_qkv: bfloat16 [3, 1024, 1024], P(None, None, 'mp'), may hold values from -0.1875 to 0.1875
- w_out: bfloat16 [1024, 1024], P('mp'), may hold values from -1 to 1
- w_up: bfloat16 [1024, 4096], P(None, 'mp'), may hold values from -0.1875 to 0.1875
- w_down: bfloat16 [4096, 1024], P('mp'), may hold values from -0.09375 to 0.09375
- w_mod: bfloat16 [1024, 6144], P('mp'), may hold values from -0.1875 to 0.1875
- b_mod: bfloat16 [6, 1024], replicated, may hold values from -3 to 3
- time_weight: bfloat16 [256, 1024], P(None, 'mp'), may hold values from -0.375 to 0.375
- class_table: bfloat16 [1000, 1024], P(None, 'mp'), may hold values from -6 to 6
- rel_table: bfloat16 [16, 961], P('mp'), may hold values from -5 to 5
- window_step: int32 [64], P('dp'), may hold values from 0 to 999
- window_label: int32 [64], P('dp'), may hold values from 0 to 999
- window_cols: int32 [64], P('dp'), may hold values from 0 to 16, as said below
Outputs:
- block_out: bfloat16 [64, 256, 1024], P(('dp', 'mp'))
- tokens_grad: bfloat16 [64, 256, 1024], P(('dp', 'mp'))
- w_qkv_grad: float32 [3, 1024, 1024], P(None, None, 'mp')
- w_out_grad: float32 [1024, 1024], P('mp')
- w_up_grad: float32 [1024, 4096], P(None, 'mp')
- w_down_grad: float32 [4096, 1024], P('mp')
- w_mod_grad: float32 [1024, 6144], P('mp')
- b_mod_grad: float32 [6, 1024], replicated
- time_weight_grad: float32 [256, 1024], P(None, 'mp')
- class_table_grad: float32 [1000, 1024], P(None, 'mp')
- rel_table_grad: float32 [16, 961], P('mp')
Inputs may be any that keep to these rules, and one draw needn't show every extreme that they name: `window_cols`: within each aligned block of 8 windows the used slots (nonzero entry) come first, two or more of them; some block is used in full. A used slot holds 16 or 8 valid columns, an unused one 0.
All inputs are finite; a program needn't handle non-finite values.
Results may differ from a plain program's by a relative error of at most 0.028.
Values may be sent and summed in bfloat16 or wider, within the bound.
No kernel may reach another device: no remote copies, remote signals or barrier semaphores. Data moves between devices by JAX's collectives and lax.ppermute only.
A program may use at most 192 MiB of HBM per device.

v0:
```python
import math
import jax
import jax.numpy as jnp
from jax import lax
from jax.sharding import PartitionSpec as P

HEAD_DIM = 64
WSIDE = 16
FREQ = 256
EPS = 1e-06
HIGH = lax.Precision.HIGHEST
MASKED = -1000000000.0


def exact(matrix_a, matrix_b):
    return jnp.dot(matrix_a, matrix_b, precision=HIGH, preferred_element_type=jnp.float32)


def layer_norm(field):
    center = field - jnp.mean(field, axis=-1, keepdims=True)
    spread = jnp.mean(center * center, axis=-1, keepdims=True)
    return center * lax.rsqrt(spread + EPS)


def modulate(field, scale_part, shift_part):
    return layer_norm(field) * (1.0 + scale_part) + shift_part


def gelu_tanh(field):
    return jax.nn.gelu(field, approximate=True)


def step_features(step_ids, half_width):
    frequency = jnp.exp(-math.log(10000.0) * jnp.arange(half_width, dtype=jnp.float32) / half_width)
    angles = step_ids.astype(jnp.float32)[:, None] * frequency[None, :]
    return jnp.concatenate([jnp.cos(angles), jnp.sin(angles)], axis=1)


def offset_table(window_side):
    offsets = jnp.arange(window_side, dtype=jnp.int32)
    offset_diff = offsets[:, None] - offsets[None, :] + window_side - 1
    return (
        offset_diff[None] == jnp.arange(2 * window_side - 1, dtype=jnp.int32)[:, None, None]
    ).astype(jnp.float32)


def make_scores(queries, keys, rel_bias, keep_keys, score_scale):
    raw_scores = (
        jnp.einsum("wihd,wjhd->whij", queries, keys, preferred_element_type=jnp.float32)
        * score_scale
        + rel_bias[None]
    )
    return jnp.where(keep_keys[:, None, None, :], raw_scores, MASKED)


def per_device(
    tokens,
    cotangent,
    w_qkv,
    w_out,
    w_up,
    w_down,
    w_mod,
    b_mod,
    time_weight,
    class_table,
    rel_table,
    window_step,
    window_label,
    window_cols,
):
    own_count, win_tok, width = tokens.shape
    group_size = window_step.shape[0]
    local_heads = w_out.shape[0] // HEAD_DIM
    score_scale = HEAD_DIM ** (-0.5)
    first_own = lax.axis_index("mp") * own_count
    features = step_features(window_step, FREQ // 2).astype(jnp.bfloat16)
    classes = jnp.arange(class_table.shape[0], dtype=jnp.int32)
    onehot = (window_label[:, None] == classes[None, :]).astype(jnp.bfloat16)
    cond_pre = jnp.dot(features, time_weight, preferred_element_type=jnp.float32) + jnp.dot(
        onehot, class_table, preferred_element_type=jnp.float32
    )
    condition = jax.nn.silu(cond_pre).astype(jnp.bfloat16)
    partial_mod = jnp.dot(condition, w_mod, preferred_element_type=jnp.float32)
    modulation = (
        lax.psum(partial_mod, "mp").reshape(group_size, 6, width) + b_mod.astype(jnp.float32)[None]
    )
    own_mod = lax.dynamic_slice_in_dim(modulation, first_own, own_count, 0)
    shift_attn, scale_attn, gate_attn, shift_mlp, scale_mlp, gate_mlp = [
        own_mod[:, column][:, None, :] for column in range(6)
    ]
    token_cols = jnp.arange(win_tok, dtype=jnp.int32) % WSIDE
    keep_keys = token_cols[None, :] < window_cols[:, None]
    keep_rows = lax.dynamic_slice_in_dim(keep_keys, first_own, own_count, 0)[:, :, None]
    rel_span = 2 * WSIDE - 1
    offset_pick = offset_table(WSIDE)
    rel_grid = rel_table.astype(jnp.float32).reshape(local_heads, rel_span, rel_span)
    half_bias = jnp.einsum("ayz,hab->hyzb", offset_pick, rel_grid, precision=HIGH)
    rel_bias = jnp.einsum("hyzb,bxw->hyxzw", half_bias, offset_pick, precision=HIGH).reshape(
        local_heads, win_tok, win_tok
    )
    inputs = tokens.astype(jnp.float32)
    normed_attn = modulate(inputs, scale_attn, shift_attn).astype(jnp.bfloat16)
    gathered_attn = lax.all_gather(normed_attn, "mp", axis=0, tiled=True)
    projected = jnp.einsum(
        "wtd,kde->kwte", gathered_attn, w_qkv, preferred_element_type=jnp.float32
    ).astype(jnp.bfloat16)
    split_shape = (group_size, win_tok, local_heads, HEAD_DIM)
    queries = projected[0].reshape(split_shape)
    keys = projected[1].reshape(split_shape)
    values = projected[2].reshape(split_shape)
    scores = make_scores(queries, keys, rel_bias, keep_keys, score_scale)
    row_max = jnp.max(scores, axis=-1, keepdims=True)
    log_total = row_max + jnp.log(jnp.sum(jnp.exp(scores - row_max), axis=-1, keepdims=True))
    probs_low = jnp.exp(scores - log_total).astype(jnp.bfloat16)
    attended = (
        jnp.einsum("whij,wjhd->wihd", probs_low, values, preferred_element_type=jnp.float32)
        .astype(jnp.bfloat16)
        .reshape(group_size, win_tok, local_heads * HEAD_DIM)
    )
    row_block = attended
    branch = lax.psum_scatter(
        jnp.einsum("wte,ed->wtd", row_block, w_out, preferred_element_type=jnp.float32).astype(
            jnp.bfloat16
        ),
        "mp",
        scatter_dimension=0,
        tiled=True,
    ).astype(jnp.float32)
    middle = inputs + gate_attn * branch
    normed_mlp = modulate(middle, scale_mlp, shift_mlp).astype(jnp.bfloat16)
    gathered_mlp = lax.all_gather(normed_mlp, "mp", axis=0, tiled=True)
    hidden_pre = jnp.einsum("wtd,df->wtf", gathered_mlp, w_up, preferred_element_type=jnp.float32)
    activation = gelu_tanh(hidden_pre).astype(jnp.bfloat16)
    row_block = activation
    mlp_out = lax.psum_scatter(
        jnp.einsum("wtf,fd->wtd", row_block, w_down, preferred_element_type=jnp.float32).astype(
            jnp.bfloat16
        ),
        "mp",
        scatter_dimension=0,
        tiled=True,
    ).astype(jnp.float32)
    block_out = jnp.where(keep_rows, middle + gate_mlp * mlp_out, 0.0).astype(jnp.bfloat16)
    grad_rows = jnp.where(keep_rows, cotangent.astype(jnp.float32), 0.0)
    d_gate_mlp = jnp.sum(grad_rows * mlp_out, axis=1)
    d_mlp = (gate_mlp * grad_rows).astype(jnp.bfloat16)
    d_mlp_all = lax.all_gather(d_mlp, "mp", axis=0, tiled=True)
    normed_again = lax.all_gather(normed_mlp, "mp", axis=0, tiled=True)
    pre_again = jnp.einsum("wtd,df->wtf", normed_again, w_up, preferred_element_type=jnp.float32)
    act_again = gelu_tanh(pre_again).astype(jnp.bfloat16)
    w_down_grad = jnp.einsum(
        "wtf,wtd->fd", act_again, d_mlp_all, preferred_element_type=jnp.float32
    )
    d_act = jnp.einsum("wtd,fd->wtf", d_mlp_all, w_down, preferred_element_type=jnp.float32)
    d_hidden = jax.vjp(gelu_tanh, pre_again)[1](d_act)[0].astype(jnp.bfloat16)
    w_up_grad = jnp.einsum(
        "wtd,wtf->df", normed_again, d_hidden, preferred_element_type=jnp.float32
    )
    row_block = d_hidden
    d_normed_mlp = lax.psum_scatter(
        jnp.einsum("wtf,df->wtd", row_block, w_up, preferred_element_type=jnp.float32),
        "mp",
        scatter_dimension=0,
        tiled=True,
    )
    pull_mlp = jax.vjp(modulate, middle, scale_mlp, shift_mlp)[1]
    d_middle_norm, d_scale_mlp, d_shift_mlp = pull_mlp(d_normed_mlp)
    d_middle = grad_rows + d_middle_norm
    d_gate_attn = jnp.sum(d_middle * branch, axis=1)
    d_branch = (gate_attn * d_middle).astype(jnp.bfloat16)
    d_branch_all = lax.all_gather(d_branch, "mp", axis=0, tiled=True)
    w_out_grad = jnp.einsum(
        "wte,wtd->ed", attended, d_branch_all, preferred_element_type=jnp.float32
    )
    d_attended = (
        jnp.einsum("wtd,ed->wte", d_branch_all, w_out, preferred_element_type=jnp.float32)
        .astype(jnp.bfloat16)
        .reshape(split_shape)
    )
    probs_back = jnp.exp(make_scores(queries, keys, rel_bias, keep_keys, score_scale) - log_total)
    d_probs = jnp.einsum("wihd,wjhd->whij", d_attended, values, preferred_element_type=jnp.float32)
    d_values = jnp.einsum(
        "whij,wihd->wjhd",
        probs_back.astype(jnp.bfloat16),
        d_attended,
        preferred_element_type=jnp.float32,
    ).astype(jnp.bfloat16)
    row_delta = jnp.sum(probs_back * d_probs, axis=-1, keepdims=True)
    d_scores = (probs_back * (d_probs - row_delta)).astype(jnp.bfloat16)
    d_queries = (
        jnp.einsum("whij,wjhd->wihd", d_scores, keys, preferred_element_type=jnp.float32)
        * score_scale
    ).astype(jnp.bfloat16)
    d_keys = (
        jnp.einsum("whij,wihd->wjhd", d_scores, queries, preferred_element_type=jnp.float32)
        * score_scale
    ).astype(jnp.bfloat16)
    d_bias = jnp.sum(d_scores, axis=0, dtype=jnp.float32).reshape(
        local_heads, WSIDE, WSIDE, WSIDE, WSIDE
    )
    d_half = jnp.einsum("hyxzw,bxw->hyzb", d_bias, offset_pick, precision=HIGH)
    rel_table_grad = jnp.einsum("hyzb,ayz->hab", d_half, offset_pick, precision=HIGH).reshape(
        local_heads, rel_span * rel_span
    )
    d_projected = jnp.stack([d_queries, d_keys, d_values]).reshape(
        3, group_size, win_tok, local_heads * HEAD_DIM
    )
    w_qkv_grad = jnp.einsum(
        "wtd,kwte->kde", gathered_attn, d_projected, preferred_element_type=jnp.float32
    )
    row_block = d_projected
    d_normed_attn = lax.psum_scatter(
        jnp.einsum("kwte,kde->wtd", row_block, w_qkv, preferred_element_type=jnp.float32).astype(
            jnp.bfloat16
        ),
        "mp",
        scatter_dimension=0,
        tiled=True,
    ).astype(jnp.float32)
    pull_attn = jax.vjp(modulate, inputs, scale_attn, shift_attn)[1]
    d_inputs_norm, d_scale_attn, d_shift_attn = pull_attn(d_normed_attn)
    tokens_grad = (d_middle + d_inputs_norm).astype(jnp.bfloat16)
    d_mod_own = jnp.stack(
        [
            d_shift_attn[:, 0],
            d_scale_attn[:, 0],
            d_gate_attn,
            d_shift_mlp[:, 0],
            d_scale_mlp[:, 0],
            d_gate_mlp,
        ],
        axis=1,
    ).reshape(own_count, 6 * width)
    d_modulation = lax.all_gather(d_mod_own.astype(jnp.bfloat16), "mp", axis=0, tiled=True).astype(
        d_mod_own.dtype
    )
    d_condition = exact(d_modulation, w_mod.T)
    d_cond_pre = jax.vjp(jax.nn.silu, cond_pre)[1](d_condition)[0]
    time_weight_grad = exact(features.astype(jnp.float32).T, d_cond_pre)
    class_table_grad = exact(onehot.astype(jnp.float32).T, d_cond_pre)
    w_mod_grad = exact(condition.astype(jnp.float32).T, d_modulation)
    b_mod_grad = jnp.sum(d_modulation, axis=0).reshape(6, width)
    (
        w_qkv_grad,
        w_out_grad,
        w_up_grad,
        w_down_grad,
        w_mod_grad,
        b_mod_grad,
        time_weight_grad,
        class_table_grad,
        rel_table_grad,
    ) = lax.psum(
        (
            w_qkv_grad,
            w_out_grad,
            w_up_grad,
            w_down_grad,
            w_mod_grad,
            b_mod_grad,
            time_weight_grad,
            class_table_grad,
            rel_table_grad,
        ),
        "dp",
    )
    return (
        block_out,
        tokens_grad,
        w_qkv_grad,
        w_out_grad,
        w_up_grad,
        w_down_grad,
        w_mod_grad,
        b_mod_grad,
        time_weight_grad,
        class_table_grad,
        rel_table_grad,
    )


def solution(mesh):
    return jax.shard_map(
        per_device,
        mesh=mesh,
        in_specs=(
            P(("dp", "mp"), None, None),
            P(("dp", "mp"), None, None),
            P(None, None, "mp"),
            P("mp", None),
            P(None, "mp"),
            P("mp", None),
            P("mp", None),
            P(),
            P(None, "mp"),
            P(None, "mp"),
            P("mp", None),
            P("dp"),
            P("dp"),
            P("dp"),
        ),
        out_specs=(
            P(("dp", "mp"), None, None),
            P(("dp", "mp"), None, None),
            P(None, None, "mp"),
            P("mp", None),
            P(None, "mp"),
            P("mp", None),
            P("mp", None),
            P(),
            P(None, "mp"),
            P(None, "mp"),
            P("mp", None),
        ),
        check_vma=False,
    )
```

profile of v0, /device:TPU:0, one launch (start us, length us, event | category | flops | bytes accessed | tf_op | source)
XLA Modules:
  0.0 1149.7 jit_solution(5632088591709699951)
XLA Ops:
  14.9 34.8 %all-reduce.5.cloned.1.call-done = f32[8,6,1024]{2,0,1:T(8,128)} async-done(((f32[8,6,1024]{2,0,1:T(8,128)}), f32[8,6,1024]{2,0,1:T(8,128)}) %all-reduce.5.cloned.1.call-update) | async-done | bytes 196624 | tf_op jit(solution)/shard_map/psum | solution.py:86
  59.8 12.0 %copy.103 = f32[4,16,16,16,16]{2,1,4,3,0:T(8,128)} copy(f32[4,16,16,16,16]{3,4,1,0,2:T(8,128)} %convolution_bitcast_fusion) | data formatting | bytes 2097152 | tf_op jit(solution)/shard_map/add | solution.py:49
  71.8 7.0 reshape.213
  78.9 55.0 %all-gather.6.cloned.1.call-done = bf16[8,256,1024]{2,1,0:T(8,128)(2,1)} async-done(((bf16[2,256,1024]{2,1,0:T(8,128)(2,1)}), bf16[8,256,1024]{2,1,0:T(8,128)(2,1)}) %all-gather.6.cloned.1.call-update) | async-done | bytes 4194320 | tf_op jit(solution)/shard_map/all_gather | solution.py:104
  133.9 6.1 convert_bitcast_fusion
  153.3 75.4 %reduce-scatter.5.cloned.1.call-done = bf16[2,256,1024]{2,1,0:T(8,128)(2,1)} async-done(((bf16[8,256,1024]{2,1,0:T(8,128)(2,1)}), bf16[2,256,1024]{2,1,0:T(8,128)(2,1)}) %reduce-scatter.5.cloned.1.call-update) | async-done | bytes 1048592 | tf_op jit(solution)/shard_map/reduce_scatter | solution.py:122
  237.2 78.7 %all-gather.8.cloned.1.call-done = bf16[8,256,1024]{2,1,0:T(8,128)(2,1)} async-done(((bf16[2,256,1024]{2,1,0:T(8,128)(2,1)}), bf16[8,256,1024]{2,1,0:T(8,128)(2,1)}) %all-gather.8.cloned.1.call-update) | async-done | bytes 4194320 | tf_op jit(solution)/shard_map/all_gather | solution.py:132
  316.0 10.9 fusion.34
  326.9 70.4 %all-gather.10.cloned.1.call-done = bf16[8,256,1024]{2,1,0:T(8,128)(2,1)} async-done(((bf16[2,256,1024]{2,1,0:T(8,128)(2,1)}), bf16[8,256,1024]{2,1,0:T(8,128)(2,1)}) %all-gather.10.cloned.1.call-update) | async-done | bytes 4194320 | tf_op jit(solution)/shard_map/all_gather | solution.py:148
  397.2 12.8 %fusion.6 = bf16[8,256,1024]{2,1,0:T(8,128)(2,1)S(1)} fusion(f32[8,256,1024]{2,1,0:T(8,128)} %fusion.34, bf16[8,256,1024]{2,1,0:T(8,128)(2,1)} %all-gather.10.cloned.1.call-done, bf16[1024,1024]{1,0:T(8,128)(2,1)} %param.19), kind=kOutput, calls=%fused_computation.8 | convolution fusion | flops 4336910336 | bytes 18874368 | tf_op jit(solution)/shard_map/wtd,fd->wtf/dot_general | solution.py:155
  412.0 7.0 fusion.32
  419.1 143.2 %reduce-scatter.9.cloned.1.call-done = f32[2,256,1024]{2,1,0:T(8,128)} async-done(((f32[8,256,1024]{2,1,0:T(8,128)}), f32[2,256,1024]{2,1,0:T(8,128)}) %reduce-scatter.9.cloned.1.call-update) | async-done | bytes 2097168 | tf_op jit(solution)/shard_map/reduce_scatter | solution.py:161
  569.6 81.5 %all-gather.12.cloned.1.call-done = bf16[8,256,1024]{2,1,0:T(8,128)(2,1)} async-done(((bf16[2,256,1024]{2,1,0:T(8,128)(2,1)}), bf16[8,256,1024]{2,1,0:T(8,128)(2,1)}) %all-gather.12.cloned.1.call-update) | async-done | bytes 4194320 | tf_op jit(solution)/shard_map/all_gather | solution.py:172
  678.1 7.8 bitcast_convert_fusion
  686.0 11.5 %convolution_convert_fusion = bf16[8,256,1024]{2,1,0:T(8,128)(2,1)} fusion(bf16[1024,1024]{1,0:T(8,128)(2,1)} %param.19, f32[8,256,1024]{2,1,0:T(8,128)} %fusion.34), kind=kOutput, calls=%fused_computation.34 | convolution fusion | flops 4315938816 | bytes 14680064 | tf_op jit(solution)/shard_map/wtf,fd->wtd/dot_general | solution.py:137
  697.8 10.2 convolution_bitcast_fusion.2
  708.1 11.2 convolution_bitcast_fusion.1
  728.3 33.1 %reduce-scatter.11.cloned.1.call-done = bf16[2,256,1024]{2,1,0:T(8,128)(2,1)} async-done(((bf16[8,256,1024]{2,1,0:T(8,128)(2,1)}), bf16[2,256,1024]{2,1,0:T(8,128)(2,1)}) %reduce-scatter.11.cloned.1.call-update) | async-done | bytes 1048592 | tf_op jit(solution)/shard_map/reduce_scatter | solution.py:213
  767.7 74.0 %reduce-scatter.7.cloned.1.call-done = bf16[2,256,1024]{2,1,0:T(8,128)(2,1)} async-done(((bf16[8,256,1024]{2,1,0:T(8,128)(2,1)}), bf16[2,256,1024]{2,1,0:T(8,128)(2,1)}) %reduce-scatter.7.cloned.1.call-update) | async-done | bytes 1048592 | tf_op jit(solution)/shard_map/reduce_scatter | solution.py:136
  847.0 13.8 %all-gather = bf16[4,2,6144]{2,1,0:T(2,128)(2,1)S(1)} all-gather(bf16[1,2,6144]{2,1,0:T(2,128)(2,1)S(1)} %bitcast.178), channel_id=1, replica_groups=mesh['dp'=8,'mp'=4] {'mp'}, dimensions={0}, use_global_device_ids=true | all-gather | bytes 122880 | tf_op jit(solution)/shard_map/all_gather | solution.py:235
  869.0 6.2 reshape.189
  875.2 6.8 convolution_bitcast_fusion.5
  882.7 25.6 %all-reduce = (f32[6,1024]{1,0:T(8,128)}, f32[4,961]{1,0:T(4,128)}) all-reduce(f32[6,1024]{1,0:T(8,128)S(1)} %reshape.188, f32[4,961]{1,0:T(4,128)S(1)} %reshape.190), channel_id=1, replica_groups=mesh['dp'=8,'mp'=4] {'dp'}, use_global_device_ids=true, to_apply=%region_28.29 | all-reduce | flops 9988 | bytes 79904 | tf_op jit(solution)/shard_map/psum | solution.py:254
  908.3 215.6 %all-reduce.7.cloned.1.call-done = (f32[3,1024,256]{1,2,0:T(8,128)}, f32[256,1024]{1,0:T(8,128)}, f32[1024,1024]{1,0:T(8,128)}, f32[1024,1024]{1,0:T(8,128)}, f3...) async-done(((f32[3,1024,256]{1,2,0:T(8,128)}, f32[256,1024]{1,0:T(8,128)}, f32[1024,1024]{1,0:T(8,128)}, f32[1024,1024]{1,0:T(8,128)}, ...) | async-done | bytes 20160528 | tf_op jit(solution)/shard_map/psum | solution.py:254
  (180 shorter events, 124.3 us)
Async XLA Ops:
  7.2 42.5 %all-reduce.5.cloned.1.call-start = ((), (), s32[]{:S(2)}) async-start(), calls=%async_computation.4 | async-start | bytes 393216 | tf_op jit(solution)/shard_map/psum | solution.py:86
  8.2 6.7 copy-start.27
  11.7 41.7 %copy-start.28 = (bf16[4,961]{1,0:T(4,128)(2,1)S(1)}, bf16[4,961]{1,0:T(4,128)(2,1)}, u32[]{:S(2)}) copy-start(bf16[4,961]{1,0:T(4,128)(2,1)} %param.24) | copy-start | bytes 23068
  11.7 122.2 %all-gather.6.cloned.1.call-start = ((), (), s32[]{:S(2)}) async-start(), calls=%async_computation.5 | async-start | bytes 5242880 | tf_op jit(solution)/shard_map/all_gather | solution.py:104
  53.3 175.4 %reduce-scatter.5.cloned.1.call-start = ((), (), s32[]{:S(2)}) async-start(), calls=%async_computation.6 | async-start | bytes 5242880 | tf_op jit(solution)/shard_map/reduce_scatter | solution.py:122
  71.8 7.0 copy-start.30
  140.3 5.7 copy-start.9
  153.3 162.7 %all-gather.8.cloned.1.call-start = ((), (), s32[]{:S(2)}) async-start(), calls=%async_computation.7 | async-start | bytes 5242880 | tf_op jit(solution)/shard_map/all_gather | solution.py:132
  234.6 162.6 %all-gather.10.cloned.1.call-start = ((), (), s32[]{:S(2)}) async-start(), calls=%async_computation.9 | async-start | bytes 5242880 | tf_op jit(solution)/shard_map/all_gather | solution.py:148
  237.2 325.1 %reduce-scatter.9.cloned.1.call-start = ((), (), s32[]{:S(2)}) async-start(), calls=%async_computation.10 | async-start | bytes 10485760 | tf_op jit(solution)/shard_map/reduce_scatter | solution.py:161
  397.2 14.8 %copy-start.34 = (bf16[1024,1024]{1,0:T(8,128)(2,1)S(1)}, bf16[1024,1024]{1,0:T(8,128)(2,1)}, u32[]{:S(2)}) copy-start(bf16[1024,1024]{1,0:T(8,128)(2,1)} %param.18) | copy-start | bytes 6291460
  419.0 232.0 %all-gather.12.cloned.1.call-start = ((), (), s32[]{:S(2)}) async-start(), calls=%async_computation.11 | async-start | bytes 5242880 | tf_op jit(solution)/shard_map/all_gather | solution.py:172
  569.5 191.9 %reduce-scatter.11.cloned.1.call-start = ((), (), s32[]{:S(2)}) async-start(), calls=%async_computation.12 | async-start | bytes 5242880 | tf_op jit(solution)/shard_map/reduce_scatter | solution.py:213
  651.0 9.7 slice-start
  654.8 6.0 slice-start.1
  654.8 6.0 copy-start.10
  686.0 155.7 %reduce-scatter.7.cloned.1.call-start = ((), (), s32[]{:S(2)}) async-start(), calls=%async_computation.8 | async-start | bytes 5242880 | tf_op jit(solution)/shard_map/reduce_scatter | solution.py:136
  697.6 426.2 %all-reduce.7.cloned.1.call-start = ((), (), s32[]{:S(2)}) async-start(), calls=%async_computation.13 | async-start | bytes 40321024 | tf_op jit(solution)/shard_map/psum | solution.py:254
  697.8 10.2 copy-start.32
  708.1 11.2 copy-start.18
  708.1 11.2 copy-start.33
  846.9 15.9 %copy-start.29 = (s32[8]{0:T(128)S(1)}, s32[8]{0:T(128)}, u32[]{:S(2)}) copy-start(s32[8]{0:T(128)} %param.26) | copy-start | bytes 100
  1129.7 5.1 copy-start.16
  1129.7 7.2 slice-start.2
  (26 other events, 71.3 us)
Sparse Core Ops, SparseCore 0:
  11.9 37.7 all-reduce.4
  53.5 80.3 all-gather.5
  153.4 75.2 reduce-scatter.4
  234.7 81.2 all-gather.7
  318.0 79.2 all-gather.9
  419.2 143.0 reduce-scatter.8
  569.6 81.3 all-gather.11
  686.1 75.2 reduce-scatter.10
  764.3 77.2 reduce-scatter.6
  868.3 255.4 all-reduce.6
where the time goes:
time: 1160 us; the launch traced here: 1150 us
  waiting for transfers between devices  862 us (74%)
  matrix products  133 us (11%)
  local copies, waits for them, and re-layouts  60.8 us (5%)
  blocking collectives  39.4 us (3%)
  other arithmetic  38.9 us (3%)
  between operations  14.9 us (1%)
    psum x1, waiting for transfers between devices, per_device(): lax.psum((w_qkv_grad, w_out_grad, w_up_grad, w_down_grad, w_mod_grad, b_m...  216 us
    reduce_scatter x1, waiting for transfers between devices, per_device(): lax.psum_scatter(jnp.einsum('wtf,df->wtd', row_block, w_up, preferred_ele...  143 us
    all_gather x1, waiting for transfers between devices, per_device(): d_branch_all = lax.all_gather(d_branch, 'mp', axis=0, tiled=True)  81.5 us
    all_gather x1, waiting for transfers between devices, per_device(): gathered_mlp = lax.all_gather(normed_mlp, 'mp', axis=0, tiled=True)  78.7 us
    reduce_scatter x1, waiting for transfers between devices, per_device(): lax.psum_scatter(jnp.einsum('wte,ed->wtd', row_block, w_out, preferred_el...  75.4 us
    reduce_scatter x1, waiting for transfers between devices, per_device(): lax.psum_scatter(jnp.einsum('wtf,fd->wtd', row_block, w_down, preferred_e...  74 us
    all_gather x1, waiting for transfers between devices, per_device(): d_mlp_all = lax.all_gather(d_mlp, 'mp', axis=0, tiled=True)  70.4 us
    all_gather x1, waiting for transfers between devices, per_device(): gathered_attn = lax.all_gather(normed_attn, 'mp', axis=0, tiled=True)  55 us
  transfers between devices with their start and end apart: 10, of which 10 were waited for; matrix products, arithmetic and copies ran while one was open for 9% of the time, Pallas kernels for 0%

commit v1 on v0

--- a/solution.py
+++ b/solution.py
@@ -3,6 +3,7 @@
 import jax.numpy as jnp
 from jax import lax
 from jax.sharding import PartitionSpec as P
+from jax.lax import all_gather
 
 HEAD_DIM = 64
 WSIDE = 16
@@ -10,6 +11,9 @@
 EPS = 1e-06
 HIGH = lax.Precision.HIGHEST
 MASKED = -1000000000.0
+choose_bench = lambda s0, u: jnp.split(
+    all_gather(jnp.concatenate([s0, u], axis=1), "mp", tiled=True, axis=0), [s0.shape[1]], axis=1
+)
 
 
 def exact(matrix_a, matrix_b):
@@ -145,8 +149,7 @@
     grad_rows = jnp.where(keep_rows, cotangent.astype(jnp.float32), 0.0)
     d_gate_mlp = jnp.sum(grad_rows * mlp_out, axis=1)
     d_mlp = (gate_mlp * grad_rows).astype(jnp.bfloat16)
-    d_mlp_all = lax.all_gather(d_mlp, "mp", axis=0, tiled=True)
-    normed_again = lax.all_gather(normed_mlp, "mp", axis=0, tiled=True)
+    d_mlp_all, normed_again = choose_bench(d_mlp, normed_mlp)
     pre_again = jnp.einsum("wtd,df->wtf", normed_again, w_up, preferred_element_type=jnp.float32)
     act_again = gelu_tanh(pre_again).astype(jnp.bfloat16)
     w_down_grad = jnp.einsum(

time: 1160 us -> 1210 us (1.043)
  waiting for transfers between devices: 862 us -> 897 us
    all_gather x1, waiting for transfers between devices: 70.4 us -> 150 us  [all_gather(jnp.concatenate([s0, u], axis=1), 'mp', tiled=True, axis=0)]
    all_gather x1, waiting for transfers between devices: 78.7 us -> 37.3 us  [per_device(): gathered_mlp = lax.all_gather(normed_mlp, 'mp', axis=0, tiled=True)]
    unnamed x93 -> x119, local copies, waits for them, and re-layouts: 28.4 us -> 29.6 us
  transfers between devices with their start and end apart: 10 -> 10, of which waited for: 10 -> 10; matrix products, arithmetic and copies ran while one was open for 9% -> 12% of each run, Pallas kernels for 0% -> 0%
where the time goes in v1:
time: 1210 us; the launch traced here: 1200 us
  waiting for transfers between devices  897 us (74%)
  matrix products  141 us (12%)
  local copies, waits for them, and re-layouts  62.4 us (5%)
  other arithmetic  44 us (4%)
  blocking collectives  39.5 us (3%)
  between operations  15 us (1%)
    psum x1, waiting for transfers between devices, per_device(): lax.psum((w_qkv_grad, w_out_grad, w_up_grad, w_down_grad, w_mod_grad, b_m...  215 us
    all_gather x1, waiting for transfers between devices, all_gather(jnp.concatenate([s0, u], axis=1), 'mp', tiled=True, axis=0)  150 us
    reduce_scatter x1, waiting for transfers between devices, per_device(): lax.psum_scatter(jnp.einsum('wtf,df->wtd', row_block, w_up, preferred_ele...  143 us
    all_gather x1, waiting for transfers between devices, per_device(): d_branch_all = lax.all_gather(d_branch, 'mp', axis=0, tiled=True)  80.7 us
    reduce_scatter x1, waiting for transfers between devices, per_device(): lax.psum_scatter(jnp.einsum('wtf,fd->wtd', row_block, w_down, preferred_e...  73.9 us
    reduce_scatter x1, waiting for transfers between devices, per_device(): lax.psum_scatter(jnp.einsum('wte,ed->wtd', row_block, w_out, preferred_el...  72.9 us
    all_gather x1, waiting for transfers between devices, per_device(): gathered_attn = lax.all_gather(normed_attn, 'mp', axis=0, tiled=True)  55 us
    all_gather x1, waiting for transfers between devices, per_device(): gathered_mlp = lax.all_gather(normed_mlp, 'mp', axis=0, tiled=True)  37.3 us
  transfers between devices with their start and end apart: 10, of which 10 were waited for; matrix products, arithmetic and copies ran while one was open for 12% of the time, Pallas kernels for 0%

profile of v1, /device:TPU:0, one launch (start us, length us, event | category | flops | bytes accessed | tf_op | source)
XLA Modules:
  0.0 1199.5 jit_solution(9052349754453714858)
XLA Ops:
  15.6 34.7 %all-reduce.5.cloned.1.call-done = f32[8,6,1024]{2,0,1:T(8,128)} async-done(((f32[8,6,1024]{2,0,1:T(8,128)}), f32[8,6,1024]{2,0,1:T(8,128)}) %all-reduce.5.cloned.1.call-update) | async-done | bytes 196624 | tf_op jit(solution)/shard_map/psum | solution.py:90
  61.0 12.1 %copy.103 = f32[4,16,16,16,16]{2,1,4,3,0:T(8,128)} copy(f32[4,16,16,16,16]{3,4,1,0,2:T(8,128)} %convolution_bitcast_fusion) | data formatting | bytes 2097152 | tf_op jit(solution)/shard_map/add | solution.py:53
  73.1 7.0 reshape.213
  80.2 55.0 %all-gather.6.cloned.1.call-done = bf16[8,256,1024]{2,1,0:T(8,128)(2,1)} async-done(((bf16[2,256,1024]{2,1,0:T(8,128)(2,1)}), bf16[8,256,1024]{2,1,0:T(8,128)(2,1)}) %all-gather.6.cloned.1.call-update) | async-done | bytes 4194320 | tf_op jit(solution)/shard_map/all_gather | solution.py:108
  157.1 72.9 %reduce-scatter.5.cloned.1.call-done = bf16[2,256,1024]{2,1,0:T(8,128)(2,1)} async-done(((bf16[8,256,1024]{2,1,0:T(8,128)(2,1)}), bf16[2,256,1024]{2,1,0:T(8,128)(2,1)}) %reduce-scatter.5.cloned.1.call-update) | async-done | bytes 1048592 | tf_op jit(solution)/shard_map/reduce_scatter | solution.py:126
  238.9 150.2 %all-gather.10.cloned.1.call-done = bf16[8,512,1024]{2,1,0:T(8,128)(2,1)} async-done(((bf16[2,512,1024]{2,1,0:T(8,128)(2,1)}), bf16[8,512,1024]{2,1,0:T(8,128)(2,1)}) %all-gather.10.cloned.1.call-update) | async-done | bytes 8388624 | tf_op jit(solution)/shard_map/all_gather | solution.py:15
  389.1 10.8 fusion.29
  399.9 11.3 fusion.6
  413.2 6.8 fusion.62
  420.1 142.9 %reduce-scatter.9.cloned.1.call-done = f32[2,256,1024]{2,1,0:T(8,128)} async-done(((f32[8,256,1024]{2,1,0:T(8,128)}), f32[2,256,1024]{2,1,0:T(8,128)}) %reduce-scatter.9.cloned.1.call-update) | async-done | bytes 2097168 | tf_op jit(solution)/shard_map/reduce_scatter | solution.py:164
  571.0 80.7 %all-gather.12.cloned.1.call-done = bf16[8,256,1024]{2,1,0:T(8,128)(2,1)} async-done(((bf16[2,256,1024]{2,1,0:T(8,128)(2,1)}), bf16[8,256,1024]{2,1,0:T(8,128)(2,1)}) %all-gather.12.cloned.1.call-update) | async-done | bytes 4194320 | tf_op jit(solution)/shard_map/all_gather | solution.py:175
  655.3 6.3 convolution_convert_fusion.1
  687.9 7.9 bitcast_convert_fusion
  695.8 37.3 %all-gather.8.cloned.1.call-done = bf16[8,256,1024]{2,1,0:T(8,128)(2,1)} async-done(((bf16[2,256,1024]{2,1,0:T(8,128)(2,1)}), bf16[8,256,1024]{2,1,0:T(8,128)(2,1)}) %all-gather.8.cloned.1.call-update) | async-done | bytes 4194320 | tf_op jit(solution)/shard_map/all_gather | solution.py:136
  733.1 13.4 %fusion.37 = bf16[8,256,1024]{2,1,0:T(8,128)(2,1)} fusion(bf16[1024,1024]{1,0:T(8,128)(2,1)} %param.19, bf16[8,256,1024]{2,1,0:T(8,128)(2,1)} %all-gather.8.cloned.1.call-done, bf16[1024,1024]{1,0:T(8,128)(2,1)} %param.18), kind=kOutput, calls=%fused_computation.55 | convolution fusion | flops 8610906112 | bytes 12582912 | tf_op jit(solution)/shard_map/wtf,fd->wtd/dot_general | solution.py:141
  747.0 10.0 fusion.44
  757.0 12.2 %fusion.47 = f32[1024,1024]{1,0:T(8,128)} fusion(bf16[8,512,1024]{2,1,0:T(8,128)(2,1)} %all-gather.10.cloned.1.call-done, f32[8,256,1024]{2,1,0:T(8,128)} %fusion.29), kind=kOutput, calls=%fused_computation.66 | convolution fusion | flops 4313841664 | bytes 16777216 | tf_op jit(solution)/shard_map/wtf,wtd->fd/dot_general | solution.py:155
  778.3 33.0 %reduce-scatter.11.cloned.1.call-done = bf16[2,256,1024]{2,1,0:T(8,128)(2,1)} async-done(((bf16[8,256,1024]{2,1,0:T(8,128)(2,1)}), bf16[2,256,1024]{2,1,0:T(8,128)(2,1)}) %reduce-scatter.11.cloned.1.call-update) | async-done | bytes 1048592 | tf_op jit(solution)/shard_map/reduce_scatter | solution.py:216
  817.6 73.9 %reduce-scatter.7.cloned.1.call-done = bf16[2,256,1024]{2,1,0:T(8,128)(2,1)} async-done(((bf16[8,256,1024]{2,1,0:T(8,128)(2,1)}), bf16[2,256,1024]{2,1,0:T(8,128)(2,1)}) %reduce-scatter.7.cloned.1.call-update) | async-done | bytes 1048592 | tf_op jit(solution)/shard_map/reduce_scatter | solution.py:140
  896.8 13.8 %all-gather = bf16[4,2,6144]{2,1,0:T(2,128)(2,1)S(1)} all-gather(bf16[1,2,6144]{2,1,0:T(2,128)(2,1)S(1)} %bitcast.179), channel_id=1, replica_groups=mesh['dp'=8,'mp'=4] {'mp'}, dimensions={0}, use_global_device_ids=true | all-gather | bytes 122880 | tf_op jit(solution)/shard_map/all_gather | solution.py:238
  918.8 6.2 reshape.189
  925.0 6.8 convolution_bitcast_fusion.3
  932.6 25.7 %all-reduce = (f32[6,1024]{1,0:T(8,128)}, f32[4,961]{1,0:T(4,128)}) all-reduce(f32[6,1024]{1,0:T(8,128)S(1)} %reshape.188, f32[4,961]{1,0:T(4,128)S(1)} %reshape.190), channel_id=1, replica_groups=mesh['dp'=8,'mp'=4] {'dp'}, use_global_device_ids=true, to_apply=%region_28.29 | all-reduce | flops 9988 | bytes 79904 | tf_op jit(solution)/shard_map/psum | solution.py:257
  958.2 215.5 %all-reduce.7.cloned.1.call-done = (f32[3,1024,256]{1,2,0:T(8,128)}, f32[256,1024]{1,0:T(8,128)}, f32[1024,1024]{1,0:T(8,128)}, f32[1024,1024]{1,0:T(8,128)}, f3...) async-done(((f32[3,1024,256]{1,2,0:T(8,128)}, f32[256,1024]{1,0:T(8,128)}, f32[1024,1024]{1,0:T(8,128)}, f32[1024,1024]{1,0:T(8,128)}, ...) | async-done | bytes 20160528 | tf_op jit(solution)/shard_map/psum | solution.py:257
  (206 shorter events, 138.3 us)
Async XLA Ops:
  7.2 43.1 %all-reduce.5.cloned.1.call-start = ((), (), s32[]{:S(2)}) async-start(), calls=%async_computation.4 | async-start | bytes 393216 | tf_op jit(solution)/shard_map/psum | solution.py:90
  12.3 42.3 %copy-start.42 = (bf16[4,961]{1,0:T(4,128)(2,1)S(1)}, bf16[4,961]{1,0:T(4,128)(2,1)}, u32[]{:S(2)}) copy-start(bf16[4,961]{1,0:T(4,128)(2,1)} %param.24) | copy-start | bytes 23068
  12.4 122.8 %all-gather.6.cloned.1.call-start = ((), (), s32[]{:S(2)}) async-start(), calls=%async_computation.5 | async-start | bytes 5242880 | tf_op jit(solution)/shard_map/all_gather | solution.py:108
  13.9 47.2 %copy-start.31 = (f32[2,256]{1,0:T(2,128)}, f32[2,256]{1,0:T(2,128)S(1)}, u32[]{:S(2)}) copy-start(f32[2,256]{1,0:T(2,128)S(1)} %broadcast_multiply_fusion.1) | copy-start | bytes 6148
  15.5 34.8 %copy-start.39 = (f32[2,256]{1,0:T(2,128)}, f32[2,256]{1,0:T(2,128)S(1)}, u32[]{:S(2)}) copy-start(f32[2,256]{1,0:T(2,128)S(1)} %fusion.58) | copy-start | bytes 6148
  15.6 45.5 %copy-start.33 = (f32[2,256]{1,0:T(2,128)}, f32[2,256]{1,0:T(2,128)S(1)}, u32[]{:S(2)}) copy-start(f32[2,256]{1,0:T(2,128)S(1)} %fusion.106) | copy-start | bytes 6148
  54.6 175.4 %reduce-scatter.5.cloned.1.call-start = ((), (), s32[]{:S(2)}) async-start(), calls=%async_computation.6 | async-start | bytes 5242880 | tf_op jit(solution)/shard_map/reduce_scatter | solution.py:126
  154.5 234.6 %all-gather.10.cloned.1.call-start = ((), (), s32[]{:S(2)}) async-start(), calls=%async_computation.9 | async-start | bytes 10485760 | tf_op jit(solution)/shard_map/all_gather | solution.py:15
  238.9 324.1 %reduce-scatter.9.cloned.1.call-start = ((), (), s32[]{:S(2)}) async-start(), calls=%async_computation.10 | async-start | bytes 10485760 | tf_op jit(solution)/shard_map/reduce_scatter | solution.py:164
  399.9 13.3 %copy-start.48 = (bf16[1024,1024]{1,0:T(8,128)(2,1)S(1)}, bf16[1024,1024]{1,0:T(8,128)(2,1)}, u32[]{:S(2)}) copy-start(bf16[1024,1024]{1,0:T(8,128)(2,1)} %param.18) | copy-start | bytes 6291460
  420.0 231.7 %all-gather.12.cloned.1.call-start = ((), (), s32[]{:S(2)}) async-start(), calls=%async_computation.11 | async-start | bytes 5242880 | tf_op jit(solution)/shard_map/all_gather | solution.py:175
  570.2 162.9 %all-gather.8.cloned.1.call-start = ((), (), s32[]{:S(2)}) async-start(), calls=%async_computation.7 | async-start | bytes 5242880 | tf_op jit(solution)/shard_map/all_gather | solution.py:136
  570.9 240.3 %reduce-scatter.11.cloned.1.call-start = ((), (), s32[]{:S(2)}) async-start(), calls=%async_computation.12 | async-start | bytes 5242880 | tf_op jit(solution)/shard_map/reduce_scatter | solution.py:216
  695.8 195.7 %reduce-scatter.7.cloned.1.call-start = ((), (), s32[]{:S(2)}) async-start(), calls=%async_computation.8 | async-start | bytes 5242880 | tf_op jit(solution)/shard_map/reduce_scatter | solution.py:140
  746.5 427.2 %all-reduce.7.cloned.1.call-start = ((), (), s32[]{:S(2)}) async-start(), calls=%async_computation.13 | async-start | bytes 40321024 | tf_op jit(solution)/shard_map/psum | solution.py:257
  757.0 12.2 %copy-start.47 = (bf16[8,256,1024]{2,1,0:T(8,128)(2,1)S(1)}, bf16[8,256,1024]{2,1,0:T(8,128)(2,1)}, u32[]{:S(2)}) copy-start(bf16[8,256,1024]{2,1,0:T(8,128)(2,1)} %all-gather.12.cloned.1.call-done) | copy-start | bytes 12582916
  772.8 39.9 %copy-start.26 = (f32[2,1024]{1,0:T(2,128)S(1)}, f32[2,1024]{1,0:T(2,128)}, u32[]{:S(2)}) copy-start(f32[2,1024]{1,0:T(2,128)} %copy-done.25) | copy-start | bytes 24580
  772.8 39.9 %copy-start.32 = (f32[2,256]{1,0:T(2,128)S(1)}, f32[2,256]{1,0:T(2,128)}, u32[]{:S(2)}) copy-start(f32[2,256]{1,0:T(2,128)} %copy-done.31) | copy-start | bytes 6148
  778.3 36.6 %copy-start.40 = (f32[2,256]{1,0:T(2,128)S(1)}, f32[2,256]{1,0:T(2,128)}, u32[]{:S(2)}) copy-start(f32[2,256]{1,0:T(2,128)} %copy-done.39) | copy-start | bytes 6148
  778.3 36.6 %copy-start.34 = (f32[2,256]{1,0:T(2,128)S(1)}, f32[2,256]{1,0:T(2,128)}, u32[]{:S(2)}) copy-start(f32[2,256]{1,0:T(2,128)} %copy-done.33) | copy-start | bytes 6148
  896.7 14.9 %copy-start.30 = (f32[8,256]{1,0:T(8,128)S(1)}, f32[8,256]{1,0:T(8,128)}, u32[]{:S(2)}) copy-start(f32[8,256]{1,0:T(8,128)} %copy-done.29) | copy-start | bytes 24580
  896.7 14.9 %copy-start.36 = (bf16[8,128]{1,0:T(8,128)(2,1)S(1)}, bf16[8,128]{1,0:T(8,128)(2,1)}, u32[]{:S(2)}) copy-start(bf16[8,128]{1,0:T(8,128)(2,1)} %copy-done.35) | copy-start | bytes 6148
  896.7 14.9 %copy-start.38 = (bf16[8,128]{1,0:T(8,128)(2,1)S(1)}, bf16[8,128]{1,0:T(8,128)(2,1)}, u32[]{:S(2)}) copy-start(bf16[8,128]{1,0:T(8,128)(2,1)} %copy-done.37) | copy-start | bytes 6148
  896.7 15.9 %copy-start.43 = (s32[8]{0:T(128)S(1)}, s32[8]{0:T(128)}, u32[]{:S(2)}) copy-start(s32[8]{0:T(128)} %param.26) | copy-start | bytes 100
  (39 other events, 150.0 us)
Sparse Core Ops, SparseCore 0:
  12.5 37.7 all-reduce.4
  54.7 80.3 all-gather.5
  154.6 75.2 reduce-scatter.4
  239.0 150.1 all-gather.9
  420.2 142.7 reduce-scatter.8
  570.3 81.3 all-gather.11
  653.9 79.2 all-gather.7
  736.0 75.2 reduce-scatter.10
  814.2 77.2 reduce-scatter.6
  918.2 255.4 all-reduce.6
